TPU v7x, 256 devices: a whole 4x4x8 slice. The times are simulated.
256 devices in a mesh: rep: 2 (over z_hi), fsdp: 32 (over y, x, core), tp: 4 (over z_lo).
Axes of the slice: x: 4, y: 4, z: 8 (z_hi: 2, z_lo: 4; z = z_hi * 4 + z_lo), core: 2. Of those that a mesh axis runs over, the one named last changes fastest.
Arguments:
- delta_out: float32 [2, 8, 1792, 1792], P('rep', None, 'tp', 'fsdp'), may hold values from -6 to 6
- delta_down: float32 [2, 8, 4864, 1792], P('rep', None, 'tp', 'fsdp'), may hold values from -6 to 6
- basis: float32 [1792, 64], replicated, may hold values from -0.125 to 0.125
- anchor_out: float32 [8, 4, 448, 1792], P('rep', 'tp', 'fsdp'), may hold values from -6 to 6
- anchor_down: float32 [8, 4, 1216, 1792], P('rep', 'tp', 'fsdp'), may hold values from -6 to 6
- moment_out: float32 [8, 4, 448, 1792], P('rep', 'tp', 'fsdp'), may hold values from -3 to 3
- moment_down: float32 [8, 4, 1216, 1792], P('rep', 'tp', 'fsdp'), may hold values from -3 to 3
Outputs:
- weights_out: bfloat16 [8, 1792, 1792], P(None, 'tp', 'fsdp')
- weights_down: bfloat16 [8, 4864, 1792], P(None, 'tp', 'fsdp')
- anchor_out_new: float32 [8, 4, 448, 1792], P('rep', 'tp', 'fsdp')
- anchor_down_new: float32 [8, 4, 1216, 1792], P('rep', 'tp', 'fsdp')
- moment_out_new: float32 [8, 4, 448, 1792], P('rep', 'tp', 'fsdp')
- moment_down_new: float32 [8, 4, 1216, 1792], P('rep', 'tp', 'fsdp')
All inputs are finite; a program needn't handle non-finite values.
Results may differ from a plain program's by a relative error of at most 0.0055.
Values may be sent and summed in bfloat16 or wider, within the bound.
A program may use at most 64 MiB of HBM per device.

v0:
```python
import jax
import jax.numpy as jnp
from jax import lax
from jax.sharding import PartitionSpec as P

outer_rate = 0.7
nesterov_decay = 0.9


def owner_update(summed, basis, anchor, moment, groups):
    coef = summed / groups
    grad = jnp.einsum("lik,jk->lij", coef, basis, precision=lax.Precision.HIGHEST)
    previous = anchor[:, 0]
    velocity = moment[:, 0]
    moment_new = nesterov_decay * velocity + grad
    anchor_new = previous - outer_rate * (grad + nesterov_decay * moment_new)
    return (anchor_new, moment_new)


def per_device(delta_out, delta_down, basis, anchor_out, anchor_down, moment_out, moment_down):
    groups = lax.axis_size("rep")
    piece_cols = delta_out.shape[3]
    shard_index = lax.axis_index("fsdp")
    basis_rows = lax.dynamic_slice_in_dim(basis, shard_index * piece_cols, piece_cols, 0)
    partial_out = jnp.einsum(
        "lij,jk->lik", delta_out[0], basis_rows, precision=lax.Precision.HIGHEST
    )
    partial_down = jnp.einsum(
        "lij,jk->lik", delta_down[0], basis_rows, precision=lax.Precision.HIGHEST
    )
    layer_sums = (
        lax.psum_scatter(
            partial_out.astype(jnp.bfloat16), "rep", scatter_dimension=0, tiled=True
        ).astype(jnp.float32),
        lax.psum_scatter(
            partial_down.astype(jnp.bfloat16), "rep", scatter_dimension=0, tiled=True
        ).astype(jnp.float32),
    )
    summed_out, summed_down = (
        lax.psum_scatter(
            layer_sums[0].astype(jnp.bfloat16), "fsdp", scatter_dimension=1, tiled=True
        ).astype(jnp.float32),
        lax.psum_scatter(
            layer_sums[1].astype(jnp.bfloat16), "fsdp", scatter_dimension=1, tiled=True
        ).astype(jnp.float32),
    )
    anchor_out_new, moment_out_new = owner_update(summed_out, basis, anchor_out, moment_out, groups)
    anchor_down_new, moment_down_new = owner_update(
        summed_down, basis, anchor_down, moment_down, groups
    )
    rounded_out = anchor_out_new.astype(jnp.bfloat16)
    rounded_down = anchor_down_new.astype(jnp.bfloat16)
    placed_out, placed_down = (
        lax.all_to_all(rounded_out, "fsdp", split_axis=2, concat_axis=1, tiled=True),
        lax.all_to_all(rounded_down, "fsdp", split_axis=2, concat_axis=1, tiled=True),
    )
    weights_out, weights_down = (
        lax.all_gather(placed_out, "rep", axis=0, tiled=True),
        lax.all_gather(placed_down, "rep", axis=0, tiled=True),
    )
    return (
        weights_out,
        weights_down,
        anchor_out_new[:, None],
        anchor_down_new[:, None],
        moment_out_new[:, None],
        moment_down_new[:, None],
    )


def solution(mesh):
    return jax.shard_map(
        per_device,
        mesh=mesh,
        in_specs=(
            P("rep", None, "tp", "fsdp"),
            P("rep", None, "tp", "fsdp"),
            P(),
            P("rep", "tp", "fsdp", None),
            P("rep", "tp", "fsdp", None),
            P("rep", "tp", "fsdp", None),
            P("rep", "tp", "fsdp", None),
        ),
        out_specs=(
            P(None, "tp", "fsdp"),
            P(None, "tp", "fsdp"),
            P("rep", "tp", "fsdp", None),
            P("rep", "tp", "fsdp", None),
            P("rep", "tp", "fsdp", None),
            P("rep", "tp", "fsdp", None),
        ),
        check_vma=False,
    )
```

profile of v0, /device:TPU:32, one launch (start us, length us, event | category | flops | bytes accessed | tf_op | source)
XLA Modules:
  0.0 316.6 jit_solution(11942777162929042482)
XLA Ops:
  7.2 0.0 copy-start
  7.2 0.0 reduce-scatter.3.cloned.1.call-start
  7.2 3.2 %fusion.2 = bf16[8,448,64]{1,2,0:T(8,128)(2,1)} fusion(f32[1,8,448,56]{2,3,1,0:T(8,128)} %param.7, f32[1792,64]{0,1:T(8,128)} %param.9, s32[]{:T(128)S(6)} %select_n.3), kind=kOutput, calls=%fused_computation.5 | convolution fusion | flops 154370048 | bytes 1409028 | tf_op jit(solution)/shard_map/lij,jk->lik/dot_general | solution.py:25
  10.4 0.0 reduce-scatter.3.cloned.1.call-update
  10.4 0.0 reduce-scatter.5.cloned.1.call-start
  10.5 0.0 copy-done
  10.5 4.2 %fusion = bf16[8,1216,64]{1,2,0:T(8,128)(2,1)} fusion(f32[1,8,1216,56]{2,3,1,0:T(8,128)S(1)} %copy-done, f32[1792,64]{0,1:T(8,128)} %param.9, s32[]{:T(128)S(6)} %select_n.3), kind=kOutput, calls=%fused_computation.1 | convolution fusion | flops 419004416 | bytes 3457028 | tf_op jit(solution)/shard_map/lij,jk->lik/dot_general | solution.py:28
  14.7 0.0 reduce-scatter.5.cloned.1.call-update
  14.7 0.0 all-reduce.5.cloned.1.call-start
  14.8 27.6 %reduce-scatter.3.cloned.1.call-done = bf16[4,448,64]{1,2,0:T(8,128)(2,1)} async-done(((bf16[8,448,64]{1,2,0:T(8,128)(2,1)}), bf16[4,448,64]{1,2,0:T(8,128)(2,1)}) %reduce-scatter.3.cloned.1.call-update) | async-done | bytes 229392 | tf_op jit(solution)/shard_map/reduce_scatter | solution.py:32
  42.3 2.0 copy.35
  44.3 43.5 %reduce-scatter.5.cloned.1.call-done = bf16[4,1216,64]{1,2,0:T(8,128)(2,1)} async-done(((bf16[8,1216,64]{1,2,0:T(8,128)(2,1)}), bf16[4,1216,64]{1,2,0:T(8,128)(2,1)}) %reduce-scatter.5.cloned.1.call-update) | async-done | bytes 622608 | tf_op jit(solution)/shard_map/reduce_scatter | solution.py:35
  87.8 3.2 %copy.43 = bf16[4,1216,64]{2,0,1:T(4,128)(2,1)} copy(bf16[4,1216,64]{1,2,0:T(8,128)(2,1)} %reduce-scatter.5.cloned.1.call-done) | data formatting | bytes 1245184 | tf_op jit(solution)/shard_map/reduce_scatter | solution.py:35
  91.0 0.0 all-reduce.5.cloned.1.call-update
  91.1 0.0 all-gather.2.cloned.1.call-start
  91.1 0.6 copy-done.4
  91.7 0.6 dynamic-slice
  93.0 112.2 %all-reduce.5.cloned.1.call-done = (bf16[4,448,64]{2,0,1:T(4,128)(2,1)}, bf16[4,1216,64]{2,0,1:T(4,128)(2,1)}) async-done(((bf16[4,448,64]{2,0,1:T(4,128)(2,1)}, bf16[4,1216,64]{2,0,1:T(4,128)(2,1)}), (bf16[4,448,64]{2,0,1:T(4,128)(2,1)}, bf16[4,1216,64]{2,0,1:T(4,128)(2,1)})) %all-reduce.5.cloned.1.call-update) | async-done | bytes 851984
  205.2 0.8 convert_multiply_fusion
  205.9 4.2 %fusion.20 = (f32[4,1,38,1792]{3,2,0,1:T(8,128)}, bf16[4,38,1792]{2,1,0:T(8,128)(2,1)}, f32[4,1,38,1792]{3,2,0,1:T(8,128)S(1)}) fusion(f32[4,1,38,1792]{3,1,2,0:T(1,128)} %param.13, f32[4,1,38,1792]{3,1,2,0:T(1,128)} %param.11, f32[1792,64]{0,1:T(8,128)} %param.9, f32[4,38,64]{2,0,1:T(4,128)S(1)} %convert_multiply_fusion), kind=kOutput, calls=%fused_computation.32 | convolution fusion | flops 211097600 | bytes 5400576 | tf_op jit(solution)/shard_map/lik,jk->lij/dot_general | solution.py:12
  210.1 3.6 %copy.46 = bf16[4,38,1792]{1,0,2:T(4,128)(2,1)} copy(bf16[4,38,1792]{2,1,0:T(8,128)(2,1)} %get-tuple-element.27) | data formatting | bytes 1089536 | tf_op jit(solution)/shard_map/convert_element_type | solution.py:52
  213.7 5.8 %reshape.22 = bf16[32,2,4256]{2,1,0:T(2,128)(2,1)} reshape(bf16[1792,4,38]{2,1,0:T(4,128)(2,1)} %bitcast.82) | data formatting | bytes 1089536
  219.4 17.7 %all_to_all.36 = bf16[32,2,4256]{2,1,0:T(2,128)(2,1)} all-to-all(bf16[32,2,4256]{2,1,0:T(2,128)(2,1)} %reshape.22), channel_id=1, replica_groups=mesh['rep'=2,'fsdp'=32,'tp'=4] {'fsdp'}, dimensions={0} | all-to-all | bytes 1089536 | tf_op jit(solution)/shard_map/all_to_all | solution.py:55
  237.2 7.4 %reshape.23 = bf16[1792,4,38]{2,1,0:T(4,128)(2,1)} reshape(bf16[32,2,4256]{2,1,0:T(2,128)(2,1)} %all_to_all.36) | data formatting | bytes 1089536
  244.6 3.5 %copy.100 = bf16[4,38,32,56]{1,2,3,0:T(8,128)(2,1)} copy(bf16[4,38,32,56]{1,0,3,2:T(4,128)(2,1)} %bitcast.80) | data formatting | bytes 1089536 | tf_op jit(solution)/shard_map/all_to_all | solution.py:55
  248.0 4.7 %all_to_all.33 = bf16[4,1216,56]{1,2,0:T(8,128)(2,1)} reshape(bf16[4,32,38,56]{2,1,3,0:T(8,128)(2,1)} %bitcast.81) | data formatting | bytes 1089536 | tf_op jit(solution)/shard_map/all_to_all | solution.py:55
  252.7 0.0 all-gather.2.cloned.1.call-update
  253.4 0.0 copy-start.1
  253.4 1.2 copy.101
  254.5 0.7 convert_multiply_fusion.1
  255.3 2.6 fusion.18
  257.9 3.3 %copy.39 = bf16[4,14,1792]{1,0,2:T(4,128)(2,1)} copy(bf16[4,14,1792]{2,1,0:T(8,128)(2,1)} %get-tuple-element.30) | data formatting | bytes 401408 | tf_op jit(solution)/shard_map/convert_element_type | solution.py:51
  261.2 4.8 %reshape.20 = bf16[32,2,1568]{2,1,0:T(2,128)(2,1)} reshape(bf16[1792,4,14]{2,1,0:T(4,128)(2,1)} %bitcast.83) | data formatting | bytes 401408
  266.1 4.8 %all-to-all-start = ((bf16[32,2,1568]{2,1,0:T(2,128)(2,1)}), bf16[32,2,1568]{2,1,0:T(2,128)(2,1)}, u32[]{:S(2)}, u32[]{:S(2)}) async-start(bf16[32,2,1568]{2,1,0:T(2,128)(2,1)} %reshape.20), calls=%async_computation.1 | async-start | bytes 425984 | tf_op jit(solution)/shard_map/all_to_all | solution.py:54
  270.8 3.4 %copy.50 = f32[4,1,38,1792]{3,1,2,0:T(1,128)} copy(f32[4,1,38,1792]{3,2,0,1:T(8,128)} %get-tuple-element.26) | data formatting | bytes 2179072
  274.2 2.1 copy.52
  276.3 0.0 copy-done.3
  276.3 1.2 copy.49
  277.5 0.0 copy-done.2
  277.5 1.2 copy.51
  278.7 0.3 all-to-all-done
  279.0 6.8 %reshape.21 = bf16[1792,4,14]{2,1,0:T(4,128)(2,1)} reshape(bf16[32,2,1568]{2,1,0:T(2,128)(2,1)} %all-to-all-done) | data formatting | bytes 401408
  285.8 3.4 %copy.53 = bf16[4,14,32,56]{3,2,0,1:T(8,128)(2,1)S(1)} copy(bf16[4,14,32,56]{1,0,3,2:T(4,128)(2,1)} %bitcast.84) | data formatting | bytes 401408 | tf_op jit(solution)/shard_map/all_to_all | solution.py:54
  289.1 0.2 copy.41
  289.4 0.3 copy.42
  289.7 17.3 %all_gather.6 = bf16[8,448,56]{1,2,0:T(8,128)(2,1)S(1)} all-gather(bf16[4,448,56]{1,2,0:T(8,128)(2,1)S(1)} %copy.42), channel_id=1, replica_groups=mesh['rep'=2,'fsdp'=32,'tp'=4] {'rep'}, dimensions={0}, use_global_device_ids=true | all-gather | bytes 602112 | tf_op jit(solution)/shard_map/all_gather | solution.py:58
  307.0 0.8 copy.106
  307.8 2.3 copy.107
  (5 shorter events, 0.0 us)
Async XLA Ops:
  7.2 3.3 %copy-start = (f32[1,8,1216,56]{2,3,1,0:T(8,128)S(1)}, f32[1,8,1216,56]{2,3,1,0:T(8,128)}, u32[]{:S(2)}) copy-start(f32[1,8,1216,56]{2,3,1,0:T(8,128)} %param.8) | copy-start | bytes 6537220
  7.2 35.2 %reduce-scatter.3.cloned.1.call-start = ((), (), s32[]{:S(2)}) async-start(), calls=%async_computation.4 | async-start | bytes 786432 | tf_op jit(solution)/shard_map/reduce_scatter | solution.py:32
  10.4 77.4 %reduce-scatter.5.cloned.1.call-start = ((), (), s32[]{:S(2)}) async-start(), calls=%async_computation.5 | async-start | bytes 1966080 | tf_op jit(solution)/shard_map/reduce_scatter | solution.py:35
  14.7 190.4 %all-reduce.5.cloned.1.call-start = ((), (), s32[]{:S(2)}) async-start(), calls=%async_computation.7 | async-start | bytes 3407872
  91.0 0.7 copy-start.4
  91.1 215.9 %all-gather.2.cloned.1.call-start = ((), (), s32[]{:S(2)}) async-start(), calls=%async_computation.6 | async-start | bytes 1720320 | tf_op jit(solution)/shard_map/all_gather | solution.py:59
  253.4 1.9 copy-start.1
  266.1 12.9 %all-to-all-start = ((bf16[32,2,1568]{2,1,0:T(2,128)(2,1)}), bf16[32,2,1568]{2,1,0:T(2,128)(2,1)}, u32[]{:S(2)}, u32[]{:S(2)}) async-start(bf16[32,2,1568]{2,1,0:T(2,128)(2,1)} %reshape.20), calls=%async_computation.1 | async-start | bytes 425984 | tf_op jit(solution)/shard_map/all_to_all | solution.py:54
  274.2 2.1 copy-start.3
  274.2 3.3 %copy-start.2 = (f32[4,1,14,1792]{3,2,0,1:T(8,128)S(1)}, f32[4,1,14,1792]{3,2,0,1:T(8,128)}, u32[]{:S(2)}) copy-start(f32[4,1,14,1792]{3,2,0,1:T(8,128)} %get-tuple-element.31) | copy-start | bytes 1204228
Sparse Core Ops, SparseCore 0:
  11.1 31.2 reduce-scatter.2
  45.0 42.7 reduce-scatter.4
  91.8 113.3 all-reduce.4
  252.8 40.9 all-gather.1
where the time goes:
time: 318 us; the launch traced here: 317 us
  waiting for transfers between devices  184 us (58%)
  local copies, waits for them, and re-layouts  62.2 us (20%)
  blocking collectives  35 us (11%)
  between operations  15.2 us (5%)
  matrix products  14.1 us (4%)
  starting transfers between devices  4.95 us (2%)
    unnamed x5, waiting for transfers between devices  112 us
    reduce_scatter x1, waiting for transfers between devices, per_device(): lax.psum_scatter(partial_down.astype(jnp.bfloat16), 'rep', scatter_dimens...  43.5 us
    unnamed x22, local copies, waits for them, and re-layouts  38 us
    reduce_scatter x1, waiting for transfers between devices, per_device(): lax.psum_scatter(partial_out.astype(jnp.bfloat16), 'rep', scatter_dimensi...  27.6 us
    all_to_all x1, blocking collectives, per_device(): lax.all_to_all(rounded_down, 'fsdp', split_axis=2, concat_axis=1, tiled=T...  17.7 us
    all_gather x1, blocking collectives, per_device(): lax.all_gather(placed_out, 'rep', axis=0, tiled=True)  17.3 us
    all_to_all x2, local copies, waits for them, and re-layouts, per_device(): lax.all_to_all(rounded_down, 'fsdp', split_axis=2, concat_axis=1, tiled=T...  8.1 us
    dot_general x2, matrix products, owner_update(): jnp.einsum('lik,jk->lij', coef, basis, precision=lax.Precision.HIGHEST)  6.77 us
  transfers between devices with their start and end apart: 5, of which 4 were waited for; matrix products, arithmetic and copies ran while one was open for 12% of the time, Pallas kernels for 0%

commit v1 on v0

--- a/solution.py
+++ b/solution.py
@@ -54,8 +54,20 @@
         lax.all_to_all(rounded_out, "fsdp", split_axis=2, concat_axis=1, tiled=True),
         lax.all_to_all(rounded_down, "fsdp", split_axis=2, concat_axis=1, tiled=True),
     )
+
+    def _press_table(view, dev_axis):
+        return jnp.concatenate(
+            lax.all_to_all(
+                jnp.stack(tuple((view for _ in range(lax.axis_size(dev_axis)))), axis=0),
+                axis_name=dev_axis,
+                split_axis=0,
+                concat_axis=0,
+            ),
+            axis=0,
+        )
+
     weights_out, weights_down = (
-        lax.all_gather(placed_out, "rep", axis=0, tiled=True),
+        _press_table(placed_out, "rep"),
         lax.all_gather(placed_down, "rep", axis=0, tiled=True),
     )
     return (

time: 318 us -> 328 us (1.031)
  blocking collectives: 35 us -> 12.9 us
  waiting for transfers between devices: 184 us -> 202 us
  starting transfers between devices: 4.95 us -> 12 us
  local copies, waits for them, and re-layouts: 62.2 us -> 67.6 us
    all_to_all x1 -> x2, waiting for transfers between devices: 0.34 us -> 18.2 us  [the longest x1 9.41 us: per_device(): lax.all_to_all(rounded_down, 'fsdp', split_axis=2, concat_axis=1, tiled=T...]
    all_gather x1 -> x0, blocking collectives: 17.3 us -> none  [per_device(): lax.all_gather(placed_out, 'rep', axis=0, tiled=True)]
    all_to_all x1 -> x2, starting transfers between devices: 4.79 us -> 11.7 us  [the longest x1 6.1 us: _press_table(): lax.all_to_all(jnp.stack(tuple((view for _ in range(lax.axis_size(dev_axi...]
    all_to_all x1, blocking collectives: 17.7 us -> 12.9 us  [per_device(): lax.all_to_all(rounded_out, 'fsdp', split_axis=2, concat_axis=1, tiled=True)]
    unnamed x22 -> x20, local copies, waits for them, and re-layouts: 38 us -> 39.8 us
  transfers between devices with their start and end apart: 5 -> 6, of which waited for: 4 -> 5; matrix products, arithmetic and copies ran while one was open for 12% -> 13% of each run, Pallas kernels for 0% -> 0%
where the time goes in v1:
time: 328 us; the launch traced here: 326 us
  waiting for transfers between devices  202 us (62%)
  local copies, waits for them, and re-layouts  67.6 us (21%)
  between operations  15.1 us (5%)
  matrix products  14.4 us (4%)
  blocking collectives  12.9 us (4%)
  starting transfers between devices  12 us (4%)
    unnamed x5, waiting for transfers between devices  112 us
    reduce_scatter x1, waiting for transfers between devices, per_device(): lax.psum_scatter(partial_down.astype(jnp.bfloat16), 'rep', scatter_dimens...  43.5 us
    unnamed x20, local copies, waits for them, and re-layouts  39.8 us
    reduce_scatter x1, waiting for transfers between devices, per_device(): lax.psum_scatter(partial_out.astype(jnp.bfloat16), 'rep', scatter_dimensi...  27.6 us
    all_to_all x1, blocking collectives, per_device(): lax.all_to_all(rounded_out, 'fsdp', split_axis=2, concat_axis=1, tiled=True)  12.9 us
    all_to_all x1, waiting for transfers between devices, per_device(): lax.all_to_all(rounded_down, 'fsdp', split_axis=2, concat_axis=1, tiled=T...  9.41 us
    all_to_all x1, waiting for transfers between devices, _press_table(): lax.all_to_all(jnp.stack(tuple((view for _ in range(lax.axis_size(dev_axi...  8.78 us
    all_to_all x2, local copies, waits for them, and re-layouts, per_device(): lax.all_to_all(rounded_down, 'fsdp', split_axis=2, concat_axis=1, tiled=T...  8.09 us
  transfers between devices with their start and end apart: 6, of which 5 were waited for; matrix products, arithmetic and copies ran while one was open for 13% of the time, Pallas kernels for 0%

profile of v1, /device:TPU:32, one launch (start us, length us, event | category | flops | bytes accessed | tf_op | source)
XLA Modules:
  0.0 326.5 jit_solution(10697939920983522356)
XLA Ops:
  7.2 0.0 copy-start
  7.2 0.0 reduce-scatter.3.cloned.1.call-start
  7.2 3.2 fusion.2
  10.4 0.0 reduce-scatter.3.cloned.1.call-update
  10.4 0.0 reduce-scatter.5.cloned.1.call-start
  10.5 0.0 copy-done
  10.5 4.2 %fusion = bf16[8,1216,64]{1,2,0:T(8,128)(2,1)} fusion(f32[1,8,1216,56]{2,3,1,0:T(8,128)S(1)} %copy-done, f32[1792,64]{0,1:T(8,128)} %param.9, s32[]{:T(128)S(6)} %select_n.3), kind=kOutput, calls=%fused_computation.1 | convolution fusion | flops 419004416 | bytes 3457028 | tf_op jit(solution)/shard_map/lij,jk->lik/dot_general | solution.py:28
  14.7 0.0 reduce-scatter.5.cloned.1.call-update
  14.7 0.0 all-reduce.5.cloned.1.call-start
  14.8 27.6 %reduce-scatter.3.cloned.1.call-done = bf16[4,448,64]{1,2,0:T(8,128)(2,1)} async-done(((bf16[8,448,64]{1,2,0:T(8,128)(2,1)}), bf16[4,448,64]{1,2,0:T(8,128)(2,1)}) %reduce-scatter.3.cloned.1.call-update) | async-done | bytes 229392 | tf_op jit(solution)/shard_map/reduce_scatter | solution.py:32
  42.3 2.0 copy.48
  44.3 43.5 %reduce-scatter.5.cloned.1.call-done = bf16[4,1216,64]{1,2,0:T(8,128)(2,1)} async-done(((bf16[8,1216,64]{1,2,0:T(8,128)(2,1)}), bf16[4,1216,64]{1,2,0:T(8,128)(2,1)}) %reduce-scatter.5.cloned.1.call-update) | async-done | bytes 622608 | tf_op jit(solution)/shard_map/reduce_scatter | solution.py:35
  87.8 3.2 copy.56
  91.0 0.0 all-reduce.5.cloned.1.call-update
  91.1 0.6 copy-done.3
  91.7 0.6 dynamic-slice
  92.9 112.2 %all-reduce.5.cloned.1.call-done = (bf16[4,448,64]{2,0,1:T(4,128)(2,1)}, bf16[4,1216,64]{2,0,1:T(4,128)(2,1)}) async-done(((bf16[4,448,64]{2,0,1:T(4,128)(2,1)}, bf16[4,1216,64]{2,0,1:T(4,128)(2,1)}), (bf16[4,448,64]{2,0,1:T(4,128)(2,1)}, bf16[4,1216,64]{2,0,1:T(4,128)(2,1)})) %all-reduce.5.cloned.1.call-update) | async-done | bytes 851984
  205.2 0.8 convert_multiply_fusion
  205.9 4.2 %fusion.20 = (f32[4,1,38,1792]{3,2,0,1:T(8,128)}, bf16[4,38,1792]{2,1,0:T(8,128)(2,1)}, f32[4,1,38,1792]{3,2,0,1:T(8,128)S(1)}) fusion(f32[4,1,38,1792]{3,1,2,0:T(1,128)} %param.13, f32[4,1,38,1792]{3,1,2,0:T(1,128)} %param.11, f32[1792,64]{0,1:T(8,128)} %param.9, f32[4,38,64]{2,0,1:T(4,128)S(1)} %convert_multiply_fusion), kind=kOutput, calls=%fused_computation.33 | convolution fusion | flops 211097600 | bytes 5400576 | tf_op jit(solution)/shard_map/lik,jk->lij/dot_general | solution.py:12
  210.1 3.6 %copy.59 = bf16[4,38,1792]{1,0,2:T(4,128)(2,1)} copy(bf16[4,38,1792]{2,1,0:T(8,128)(2,1)} %get-tuple-element.33) | data formatting | bytes 1089536 | tf_op jit(solution)/shard_map/convert_element_type | solution.py:52
  213.7 5.8 %reshape.27 = bf16[32,2,4256]{2,1,0:T(2,128)(2,1)} reshape(bf16[1792,4,38]{2,1,0:T(4,128)(2,1)} %bitcast.83) | data formatting | bytes 1089536
  219.4 5.6 %all-to-all-start.2 = ((bf16[32,2,4256]{2,1,0:T(2,128)(2,1)}), bf16[32,2,4256]{2,1,0:T(2,128)(2,1)}, u32[]{:S(2)}, u32[]{:S(2)}) async-start(bf16[32,2,4256]{2,1,0:T(2,128)(2,1)} %reshape.27), calls=%async_computation.4 | async-start | bytes 1114112 | tf_op jit(solution)/shard_map/all_to_all | solution.py:55
  225.0 0.2 all-gather.2.cloned.1.call-start
  225.9 1.9 copy.114
  227.8 9.4 %all-to-all-done.2 = bf16[32,2,4256]{2,1,0:T(2,128)(2,1)} async-done(((bf16[32,2,4256]{2,1,0:T(2,128)(2,1)}), bf16[32,2,4256]{2,1,0:T(2,128)(2,1)}, u32[]{:S(2)}, u32[]{:S(2)}) %all-to-all-start.2) | async-done | bytes 544800 | tf_op jit(solution)/shard_map/all_to_all | solution.py:55
  237.2 7.4 %reshape.28 = bf16[1792,4,38]{2,1,0:T(4,128)(2,1)} reshape(bf16[32,2,4256]{2,1,0:T(2,128)(2,1)} %all-to-all-done.2) | data formatting | bytes 1089536
  244.6 3.4 %copy.113 = bf16[4,38,32,56]{1,2,3,0:T(8,128)(2,1)} copy(bf16[4,38,32,56]{1,0,3,2:T(4,128)(2,1)} %bitcast.81) | data formatting | bytes 1089536 | tf_op jit(solution)/shard_map/all_to_all | solution.py:55
  248.0 4.6 %all_to_all.34 = bf16[4,1216,56]{1,2,0:T(8,128)(2,1)} reshape(bf16[4,32,38,56]{2,1,3,0:T(8,128)(2,1)} %bitcast.82) | data formatting | bytes 1089536 | tf_op jit(solution)/shard_map/all_to_all | solution.py:55
  252.7 0.0 all-gather.2.cloned.1.call-update
  252.7 0.7 convert_multiply_fusion.1
  253.4 2.9 fusion.18
  256.3 3.3 %copy.52 = bf16[4,14,1792]{1,0,2:T(4,128)(2,1)} copy(bf16[4,14,1792]{2,1,0:T(8,128)(2,1)} %get-tuple-element.36) | data formatting | bytes 401408 | tf_op jit(solution)/shard_map/convert_element_type | solution.py:51
  259.6 4.8 %reshape.25 = bf16[32,2,1568]{2,1,0:T(2,128)(2,1)} reshape(bf16[1792,4,14]{2,1,0:T(4,128)(2,1)} %bitcast.84) | data formatting | bytes 401408
  264.4 12.9 %all_to_all.38 = bf16[32,2,1568]{2,1,0:T(2,128)(2,1)} all-to-all(bf16[32,2,1568]{2,1,0:T(2,128)(2,1)} %reshape.25), channel_id=1, replica_groups=mesh['rep'=2,'fsdp'=32,'tp'=4] {'fsdp'}, dimensions={0} | all-to-all | bytes 401408 | tf_op jit(solution)/shard_map/all_to_all | solution.py:54
  277.3 6.8 %reshape.26 = bf16[1792,4,14]{2,1,0:T(4,128)(2,1)} reshape(bf16[32,2,1568]{2,1,0:T(2,128)(2,1)} %all_to_all.38) | data formatting | bytes 401408
  284.1 4.2 %copy.66 = bf16[4,14,32,56]{3,2,0,1:T(8,128)(2,1)} copy(bf16[4,14,32,56]{1,0,3,2:T(4,128)(2,1)} %bitcast.85) | data formatting | bytes 401408 | tf_op jit(solution)/shard_map/all_to_all | solution.py:54
  288.2 1.3 copy.54
  289.5 1.4 pad_maximum_fusion
  290.9 2.2 copy.55
  293.1 6.1 %all-to-all-start.1 = ((bf16[2,4,448,56]{2,3,1,0:T(8,128)(2,1)}), bf16[2,4,448,56]{2,3,1,0:T(8,128)(2,1)}, u32[]{:S(2)}, u32[]{:S(2)}) async-start(bf16[2,4,448,56]{2,3,1,0:T(8,128)(2,1)} %copy.55), calls=%async_computation.2 | async-start | bytes 917504 | tf_op jit(solution)/shard_map/all_to_all | solution.py:60
  299.2 3.4 %copy.63 = f32[4,1,38,1792]{3,1,2,0:T(1,128)} copy(f32[4,1,38,1792]{3,2,0,1:T(8,128)} %get-tuple-element.32) | data formatting | bytes 2179072
  302.5 2.1 copy.65
  304.7 0.0 copy-done.2
  304.7 1.2 copy.62
  305.8 1.2 copy.64
  307.0 8.8 %all-to-all-done.1 = bf16[2,4,448,56]{2,3,1,0:T(8,128)(2,1)} async-done(((bf16[2,4,448,56]{2,3,1,0:T(8,128)(2,1)}), bf16[2,4,448,56]{2,3,1,0:T(8,128)(2,1)}, u32[]{:S(2)}, u32[]{:S(2)}) %all-to-all-start.1) | async-done | bytes 401440 | tf_op jit(solution)/shard_map/all_to_all | solution.py:60
  315.8 1.8 copy.119
  317.6 2.3 copy.120
  (5 shorter events, 0.0 us)
Async XLA Ops:
  7.2 3.3 %copy-start = (f32[1,8,1216,56]{2,3,1,0:T(8,128)S(1)}, f32[1,8,1216,56]{2,3,1,0:T(8,128)}, u32[]{:S(2)}) copy-start(f32[1,8,1216,56]{2,3,1,0:T(8,128)} %param.8) | copy-start | bytes 6537220
  7.2 35.2 %reduce-scatter.3.cloned.1.call-start = ((), (), s32[]{:S(2)}) async-start(), calls=%async_computation.5 | async-start | bytes 786432 | tf_op jit(solution)/shard_map/reduce_scatter | solution.py:32
  10.4 77.4 %reduce-scatter.5.cloned.1.call-start = ((), (), s32[]{:S(2)}) async-start(), calls=%async_computation.6 | async-start | bytes 1966080 | tf_op jit(solution)/shard_map/reduce_scatter | solution.py:35
  14.7 190.4 %all-reduce.5.cloned.1.call-start = ((), (), s32[]{:S(2)}) async-start(), calls=%async_computation.8 | async-start | bytes 3407872
  91.0 0.7 copy-start.3
  219.4 17.7 %all-to-all-start.2 = ((bf16[32,2,4256]{2,1,0:T(2,128)(2,1)}), bf16[32,2,4256]{2,1,0:T(2,128)(2,1)}, u32[]{:S(2)}, u32[]{:S(2)}) async-start(bf16[32,2,4256]{2,1,0:T(2,128)(2,1)} %reshape.27), calls=%async_computation.4 | async-start | bytes 1114112 | tf_op jit(solution)/shard_map/all_to_all | solution.py:55
  225.0 90.7 %all-gather.2.cloned.1.call-start = ((), (), s32[]{:S(2)}) async-start(), calls=%async_computation.7 | async-start | bytes 1720320 | tf_op jit(solution)/shard_map/all_gather | solution.py:71
  293.1 22.7 %all-to-all-start.1 = ((bf16[2,4,448,56]{2,3,1,0:T(8,128)(2,1)}), bf16[2,4,448,56]{2,3,1,0:T(8,128)(2,1)}, u32[]{:S(2)}, u32[]{:S(2)}) async-start(bf16[2,4,448,56]{2,3,1,0:T(8,128)(2,1)} %copy.55), calls=%async_computation.2 | async-start | bytes 917504 | tf_op jit(solution)/shard_map/all_to_all | solution.py:60
  302.5 2.1 copy-start.2
  302.5 3.3 %copy-start.1 = (f32[4,1,14,1792]{3,2,0,1:T(8,128)S(1)}, f32[4,1,14,1792]{3,2,0,1:T(8,128)}, u32[]{:S(2)}) copy-start(f32[4,1,14,1792]{3,2,0,1:T(8,128)} %get-tuple-element.37) | copy-start | bytes 1204228
Sparse Core Ops, SparseCore 0:
  11.1 31.2 reduce-scatter.2
  45.0 42.7 reduce-scatter.4
  91.8 113.3 all-reduce.4
  252.8 40.9 all-gather.1
